TPU v7x, 32 devices: a whole 2x2x4 slice. The times are simulated.
32 devices in a mesh: batch: 4 (over x, core), lat: 4 (over z), lon: 2 (over y).
Axes of the slice: x: 2, y: 2, z: 4, core: 2. Of those that a mesh axis runs over, the one named last changes fastest.
Arguments:
- tokens: bfloat16 [4, 2, 48, 48, 1024], P('batch', None, 'lat', 'lon'), may hold values from -6 to 6
- weights: bfloat16 [1024, 4096], P('batch')
- regions: int32 [2, 48, 48], P(None, 'lat', 'lon'), may hold values from 0 to 3
- offsets: int32 [2], replicated, may hold values from 1 to 11, as said below
Outputs:
- mixed: bfloat16 [4, 2, 48, 48, 1024], P('batch', None, 'lat', 'lon')
Inputs may be any that keep to these rules, and one draw needn't show every extreme that they name: `offsets`: element 0 lies from 1 to 5; element 1 equals 11.
All inputs are finite; a program needn't handle non-finite values.
Results may differ from a plain program's by a relative error of at most 0.0042.
Values may be sent and summed in bfloat16 or wider, within the bound.
A program may use at most 128 MiB of HBM per device.

v0:
```python
import jax
import jax.numpy as jnp
from jax import lax
from jax.sharding import PartitionSpec as P

HEADS = 16
WLEV = 2
WLAT = 6
WLON = 12


def from_behind(block, axis, distance):
    devices = range(lax.axis_size(axis))
    route = [((i - distance) % len(devices), i) for i in devices]
    return lax.ppermute(block, axis, route)


def layer_norm(field):
    field = field.astype(jnp.float32)
    average = jnp.mean(field, -1, keepdims=True)
    centred = field - average
    variance = jnp.mean(centred * centred, -1, keepdims=True)
    return (centred * lax.rsqrt(variance + 1e-05)).astype(jnp.bfloat16)


def windows(field):
    levels, rows_lat, cols_lon, features = field.shape
    field = field.reshape(
        levels // WLEV, WLEV, rows_lat // WLAT, WLAT, cols_lon // WLON, WLON, features
    )
    field = field.transpose(0, 2, 4, 1, 3, 5, 6)
    return field.reshape(-1, WLEV * WLAT * WLON, features)


def unwindows(field, levels, rows_lat, cols_lon):
    features = field.shape[-1]
    field = field.reshape(
        levels // WLEV, rows_lat // WLAT, cols_lon // WLON, WLEV, WLAT, WLON, features
    )
    field = field.transpose(0, 3, 1, 4, 2, 5, 6)
    return field.reshape(levels, rows_lat, cols_lon, features)


def attend(normed, all_weights, regions):
    levels, rows_lat, cols_lon, width = normed.shape
    qkv = jnp.dot(
        normed.reshape(-1, width), all_weights[:, : 3 * width], preferred_element_type=jnp.float32
    ).astype(jnp.bfloat16)
    qkv = windows(qkv.reshape(levels, rows_lat, cols_lon, 3 * width))
    num_windows, win_size = (qkv.shape[0], qkv.shape[1])
    head_size = width // HEADS
    queries = qkv[..., :width].reshape(num_windows, win_size, HEADS, head_size)
    keys_all = qkv[..., width : 2 * width].reshape(num_windows, win_size, HEADS, head_size)
    values_all = qkv[..., 2 * width :].reshape(num_windows, win_size, HEADS, head_size)
    scores = jnp.einsum(
        "wqhe,wkhe->whqk", queries, keys_all, preferred_element_type=jnp.float32
    ) * head_size ** (-0.5)
    region_ids = windows(regions[..., None])[..., 0]
    allowed = region_ids[:, None, :, None] == region_ids[:, None, None, :]
    scores = jnp.where(allowed, scores, -1e30)
    largest = jnp.max(scores, -1, keepdims=True)
    expsc = jnp.exp(scores - largest)
    attn_probs = (expsc / jnp.sum(expsc, -1, keepdims=True)).astype(jnp.bfloat16)
    mixed_out = jnp.einsum(
        "whqk,wkhe->wqhe", attn_probs, values_all, preferred_element_type=jnp.float32
    )
    mixed_out = mixed_out.astype(jnp.bfloat16).reshape(num_windows, win_size, width)
    return unwindows(mixed_out, levels, rows_lat, cols_lon)


def roll_forward(block_in, offsets):
    rows_lat, cols_lon = (block_in.shape[1], block_in.shape[2])
    from_next = from_behind(block_in[:, :WLAT], "lat", -1)
    joined = jnp.concatenate([block_in, from_next], axis=1)
    block_in = lax.dynamic_slice_in_dim(joined, offsets[0], rows_lat, 1)
    from_next = from_behind(block_in[:, :, :WLON], "lon", -1)
    joined = jnp.concatenate([block_in, from_next], axis=2)
    return lax.dynamic_slice_in_dim(joined, offsets[1], cols_lon, 2)


def roll_back(block_in, offsets):
    rows_lat, cols_lon = (block_in.shape[1], block_in.shape[2])
    from_prev = from_behind(block_in[:, rows_lat - WLAT :], "lat", 1)
    joined = jnp.concatenate([from_prev, block_in], axis=1)
    block_in = lax.dynamic_slice_in_dim(joined, WLAT - offsets[0], rows_lat, 1)
    from_prev = from_behind(block_in[:, :, cols_lon - WLON :], "lon", 1)
    joined = jnp.concatenate([from_prev, block_in], axis=2)
    return lax.dynamic_slice_in_dim(joined, WLON - offsets[1], cols_lon, 2)


def local(tokens, weights, regions, offsets):
    width = weights.shape[1] // 4
    all_weights = lax.all_gather(weights, "batch", axis=0, tiled=True)
    block_in = tokens[0]
    rolled = roll_forward(block_in, offsets)
    attended = attend(layer_norm(rolled), all_weights, regions)
    back_rolled = roll_back(attended, offsets)
    projected = jnp.dot(
        back_rolled.reshape(-1, width),
        all_weights[:, 3 * width :],
        preferred_element_type=jnp.float32,
    )
    mixed = block_in.astype(jnp.float32) + projected.reshape(block_in.shape)
    return mixed.astype(jnp.bfloat16)[None]


def solution(mesh):
    in_specs = (P("batch", None, "lat", "lon", None), P("batch", None), P(None, "lat", "lon"), P())
    out_specs = P("batch", None, "lat", "lon", None)
    return jax.shard_map(local, mesh=mesh, in_specs=in_specs, out_specs=out_specs, check_vma=False)
```

profile of v0, /device:TPU:0, one launch (start us, length us, event | category | flops | bytes accessed | tf_op | source)
XLA Modules:
  0.0 174.3 jit_solution(2364879644640626707)
XLA Ops:
  6.5 0.7 all-gather.2.cloned.1.call-update
  7.3 0.5 copy-done.2
  7.8 5.1 %collective-permute-start = (bf16[2,6,24,1024]{3,2,1,0:T(8,128)(2,1)S(1)}, bf16[2,6,24,1024]{3,2,1,0:T(8,128)(2,1)S(1)}, u32[]{:S(2)}, u32[]{:S(2)}) collective-permute-start(bf16[2,6,24,1024]{3,2,1,0:T(8,128)(2,1)S(1)} %slice.46), channel_id=1, source_target_pairs={{2,0},{4,2},{6,4},{0,6},{3,1},{5,3},{7,5},{1,7},{10,8},{12,10},{14... | collective-permute-start | bytes 1769480 | tf_op jit(solution)/shard_map/ppermute | solution.py:15
  13.0 0.6 fusion.30
  15.6 9.9 %collective-permute-done = bf16[2,6,24,1024]{3,2,1,0:T(8,128)(2,1)S(1)} collective-permute-done((bf16[2,6,24,1024]{3,2,1,0:T(8,128)(2,1)S(1)}, bf16[2,6,24,1024]{3,2,1,0:T(8,128)(2,1)S(1)}, u32[]{:S(2)}, u32[]{:S(2)}) %collective-permute-start) | collective-permute-done | bytes 589856 | tf_op jit(solution)/shard_map/ppermute | solution.py:15
  26.0 0.6 copy.17
  26.6 1.6 collective-permute-start.1
  30.1 0.8 broadcast_compare_fusion
  30.9 9.9 %collective-permute-done.1 = bf16[2,12,12,1024]{3,0,2,1:T(2,128)(2,1)S(1)} collective-permute-done((bf16[2,12,12,1024]{3,0,2,1:T(2,128)(2,1)S(1)}, bf16[2,12,12,1024]{3,0,2,1:T(2,128)(2,1)S(1)}, u32[]{:S(2)}, u32[]{:S(2)}) %collective-permute-start.1) | collective-permute-done | bytes 589856 | tf_op jit(solution)/shard_map/ppermute | solution.py:15
  41.0 1.1 convert_reduce_fusion
  42.1 0.4 fusion.13
  42.5 1.4 fusion.14
  43.9 26.1 %all-gather.2.cloned.1.call-done = bf16[1024,4096]{1,0:T(8,128)(2,1)} async-done(((bf16[256,4096]{1,0:T(8,128)(2,1)}), bf16[1024,4096]{1,0:T(8,128)(2,1)}) %all-gather.2.cloned.1.call-update) | async-done | bytes 8388624 | tf_op jit(solution)/shard_map/all_gather | solution.py:93
  69.9 7.0 %fusion.8 = bf16[576,3072]{1,0:T(8,128)(2,1)S(1)} fusion(bf16[576,1024]{1,0:T(8,128)(2,1)} %bitcast.51, bf16[1024,4096]{1,0:T(8,128)(2,1)} %all-gather.2.cloned.1.call-done), kind=kOutput, calls=%fused_computation.11 | convolution fusion | flops 3625648128 | bytes 11010048 | tf_op jit(solution)/shard_map/dot_general | solution.py:46
  76.9 3.5 %reshape_reshape.6 = bf16[1,2,2,6,2,12,3072]{6,5,4,3,2,1,0:T(8,128)(2,1)} reshape(bf16[576,3072]{1,0:T(8,128)(2,1)S(1)} %fusion.8) | data formatting | bytes 7077888 | tf_op jit(solution)/shard_map/reshape;reshape | solution.py:28
  80.5 7.8 %copy.19 = bf16[1,2,2,2,6,12,3072]{6,2,1,5,4,3,0:T(2,128)(2,1)} copy(bf16[1,2,2,2,6,12,3072]{6,5,2,4,1,3,0:T(8,128)(2,1)} %bitcast.43) | data formatting | bytes 7077888 | tf_op jit(solution)/shard_map/transpose | solution.py:31
  88.2 7.7 %reshape.45 = bf16[4,144,3072]{2,0,1:T(4,128)(2,1)S(1)} reshape(bf16[1,2,2,2,6,12,3072]{6,2,1,5,4,3,0:T(2,128)(2,1)} %copy.19) | data formatting | bytes 7077888 | tf_op jit(solution)/shard_map/reshape | solution.py:32
  95.9 2.7 %fusion.29 = (bf16[4,144,1024]{2,0,1:T(4,128)(2,1)}, bf16[4,144,1024]{2,0,1:T(4,128)(2,1)}, bf16[4,144,1024]{2,0,1:T(4,128)(2,1)}) fusion(bf16[4,144,3072]{2,0,1:T(4,128)(2,1)S(1)} %reshape.45), kind=kLoop, calls=%fused_computation.44 | loop fusion | bytes 7077888 | tf_op jit(solution)/shard_map/slice | solution.py:53
  98.6 4.1 %copy.22 = bf16[4,144,1024]{1,2,0:T(8,128)(2,1)} copy(bf16[4,144,1024]{2,0,1:T(4,128)(2,1)} %get-tuple-element.8) | data formatting | bytes 2359296 | tf_op jit(solution)/shard_map/slice | solution.py:52
  102.7 2.5 %copy.23 = bf16[4,144,1024]{1,2,0:T(8,128)(2,1)} copy(bf16[4,144,1024]{2,0,1:T(4,128)(2,1)S(1)} %copy-done.1) | data formatting | bytes 2359296 | tf_op jit(solution)/shard_map/slice | solution.py:53
  105.1 2.5 %copy.20 = bf16[4,144,1024]{1,2,0:T(8,128)(2,1)} copy(bf16[4,144,1024]{2,0,1:T(4,128)(2,1)S(1)} %copy-done) | data formatting | bytes 2359296 | tf_op jit(solution)/shard_map/slice | solution.py:54
  107.6 8.8 %fusion.31 = (f32[4,16,144]{2,1,0:T(8,128)S(1)}, f32[4,16,144,144]{2,3,1,0:T(8,128)}) fusion(pred[4,144,144]{1,2,0:T(8,128)(4,1)S(1)} %copy-done.5, bf16[4,144,16,64]{1,3,2,0:T(8,128)(2,1)S(1)} %bitcast.48, bf16[4,144,16,64]{1,3,2,0:T(8,128)(2,1)} %bitcast.49), kind=kOutput, calls=%fused_computation.46 | convolution fusion | flops 175177872 | bytes 7787520 | tf_op jit(solution)/shard_map/sub | solution.py:62
  116.4 6.5 %convert_bitcast_fusion = bf16[4,144,16,64]{1,3,2,0:T(8,128)(2,1)} fusion(bf16[4,144,16,64]{1,3,2,0:T(8,128)(2,1)} %bitcast.50, f32[4,16,144,144]{2,3,1,0:T(8,128)} %get-tuple-element.13, f32[4,16,144]{2,1,0:T(8,128)S(1)} %get-tuple-element.12), kind=kOutput, calls=%fused_computation.21 | convolution fusion | flops 173113344 | bytes 7704576 | tf_op jit(solution)/shard_map/whqk,wkhe->wqhe/dot_general | solution.py:64
  123.0 3.8 %copy.25 = bf16[4,144,16,64]{3,2,0,1:T(8,128)(2,1)S(1)} copy(bf16[4,144,16,64]{1,3,2,0:T(8,128)(2,1)} %convert_bitcast_fusion) | data formatting | bytes 2359296 | tf_op jit(solution)/shard_map/convert_element_type | solution.py:67
  126.8 1.4 reshape_reshape.7
  128.2 1.2 copy.26
  129.8 1.5 collective-permute-start.2
  132.7 14.4 %collective-permute-done.2 = bf16[2,6,24,1024]{3,2,1,0:T(8,128)(2,1)S(1)} collective-permute-done((bf16[2,6,24,1024]{3,2,1,0:T(8,128)(2,1)S(1)}, bf16[2,6,24,1024]{3,2,1,0:T(8,128)(2,1)S(1)}, u32[]{:S(2)}, u32[]{:S(2)}) %collective-permute-start.2) | collective-permute-done | bytes 589856 | tf_op jit(solution)/shard_map/ppermute | solution.py:15
  147.6 0.6 copy.29
  148.2 1.5 collective-permute-start.3
  150.9 12.1 %collective-permute-done.3 = bf16[2,12,12,1024]{3,0,2,1:T(2,128)(2,1)S(1)} collective-permute-done((bf16[2,12,12,1024]{3,0,2,1:T(2,128)(2,1)S(1)}, bf16[2,12,12,1024]{3,0,2,1:T(2,128)(2,1)S(1)}, u32[]{:S(2)}, u32[]{:S(2)}) %collective-permute-start.3) | collective-permute-done | bytes 589856 | tf_op jit(solution)/shard_map/ppermute | solution.py:15
  163.2 4.3 %fusion.16 = bf16[1,2,12,24,1024]{4,3,2,1,0:T(8,128)(2,1)} fusion(bf16[1024,4096]{1,0:T(8,128)(2,1)} %all-gather.2.cloned.1.call-done, s32[]{:T(128)S(6)} %select_n.20, bf16[2,12,12,1024]{3,2,1,0:T(8,128)(2,1)S(1)} %copy.30, bf16[2,12,24,1024]{3,2,1,0:T(8,128)(2,1)S(1)} %fusion.17, bf16[1,2,12,24,1024]{4,3,2,1,0:T(8,128)(2,1)S(1)} %copy-done.3), kind=kOutput, calls=%fused_computation.30 | convolution fusion | flops 1212088320 | bytes 6225924 | tf_op jit(solution)/shard_map/dot_general | solution.py:98
  (30 shorter events, 1.8 us)
Async XLA Ops:
  6.5 1.3 copy-start.2
  6.5 6.4 %copy-start.7 = (s32[2]{0:T(128)S(1)}, s32[2]{0:T(128)}, u32[]{:S(2)}) copy-start(s32[2]{0:T(128)} %param.7) | copy-start | bytes 28
  6.5 63.4 %all-gather.2.cloned.1.call-start = ((), (), s32[]{:S(2)}) async-start(), calls=%async_computation | async-start | bytes 10485760 | tf_op jit(solution)/shard_map/all_gather | solution.py:93
  7.8 17.7 %collective-permute-start = (bf16[2,6,24,1024]{3,2,1,0:T(8,128)(2,1)S(1)}, bf16[2,6,24,1024]{3,2,1,0:T(8,128)(2,1)S(1)}, u32[]{:S(2)}, u32[]{:S(2)}) collective-permute-start(bf16[2,6,24,1024]{3,2,1,0:T(8,128)(2,1)S(1)} %slice.46), channel_id=1, source_target_pairs={{2,0},{4,2},{6,4},{0,6},{3,1},{5,3},{7,5},{1,7},{10,8},{12,10},{14... | collective-permute-start | bytes 1769480 | tf_op jit(solution)/shard_map/ppermute | solution.py:15
  25.9 3.4 %copy-start.6 = (s32[2,12,24]{2,0,1:T(2,128)S(1)}, s32[2,12,24]{2,0,1:T(2,128)}, u32[]{:S(2)}) copy-start(s32[2,12,24]{2,0,1:T(2,128)} %param.6) | copy-start | bytes 6916
  26.6 14.3 %collective-permute-start.1 = (bf16[2,12,12,1024]{3,0,2,1:T(2,128)(2,1)S(1)}, bf16[2,12,12,1024]{3,0,2,1:T(2,128)(2,1)S(1)}, u32[]{:S(2)}, u32[]{:S(2)}) collective-permute-start(bf16[2,12,12,1024]{3,0,2,1:T(2,128)(2,1)S(1)} %copy.17), channel_id=1, source_target_pairs={{1,0},{0,1},{3,2},{2,3},{5,4},{4,5},{7,6},{6,7},{9,8},{8,9},{11,10... | collective-permute-start | bytes 1769480 | tf_op jit(solution)/shard_map/ppermute | solution.py:15
  98.6 4.1 %copy-start.1 = (bf16[4,144,1024]{2,0,1:T(4,128)(2,1)S(1)}, bf16[4,144,1024]{2,0,1:T(4,128)(2,1)}, u32[]{:S(2)}) copy-start(bf16[4,144,1024]{2,0,1:T(4,128)(2,1)} %get-tuple-element.7) | copy-start | bytes 3538948
  102.7 2.5 %copy-start = (bf16[4,144,1024]{2,0,1:T(4,128)(2,1)S(1)}, bf16[4,144,1024]{2,0,1:T(4,128)(2,1)}, u32[]{:S(2)}) copy-start(bf16[4,144,1024]{2,0,1:T(4,128)(2,1)} %get-tuple-element.9) | copy-start | bytes 3538948
  105.1 2.5 %copy-start.4 = (bf16[4,144,1024]{1,2,0:T(8,128)(2,1)S(1)}, bf16[4,144,1024]{1,2,0:T(8,128)(2,1)}, u32[]{:S(2)}) copy-start(bf16[4,144,1024]{1,2,0:T(8,128)(2,1)} %copy.22) | copy-start | bytes 3538948
  105.1 2.5 %copy-start.5 = (pred[4,144,144]{1,2,0:T(8,128)(4,1)S(1)}, pred[4,144,144]{1,2,0:T(8,128)(4,1)}, u32[]{:S(2)}) copy-start(pred[4,144,144]{1,2,0:T(8,128)(4,1)} %broadcast_compare_fusion) | copy-start | bytes 248836
  129.8 17.3 %collective-permute-start.2 = (bf16[2,6,24,1024]{3,2,1,0:T(8,128)(2,1)S(1)}, bf16[2,6,24,1024]{3,2,1,0:T(8,128)(2,1)S(1)}, u32[]{:S(2)}, u32[]{:S(2)}) collective-permute-start(bf16[2,6,24,1024]{3,2,1,0:T(8,128)(2,1)S(1)} %slice.52), channel_id=1, source_target_pairs={{6,0},{0,2},{2,4},{4,6},{7,1},{1,3},{3,5},{5,7},{14,8},{8,10},{10,... | collective-permute-start | bytes 1769480 | tf_op jit(solution)/shard_map/ppermute | solution.py:15
  147.4 15.8 %copy-start.3 = (bf16[1,2,12,24,1024]{4,3,2,1,0:T(8,128)(2,1)S(1)}, bf16[1,2,12,24,1024]{4,3,2,1,0:T(8,128)(2,1)}, u32[]{:S(2)}) copy-start(bf16[1,2,12,24,1024]{4,3,2,1,0:T(8,128)(2,1)} %param.4) | copy-start | bytes 3538948
  148.2 14.8 %collective-permute-start.3 = (bf16[2,12,12,1024]{3,0,2,1:T(2,128)(2,1)S(1)}, bf16[2,12,12,1024]{3,0,2,1:T(2,128)(2,1)S(1)}, u32[]{:S(2)}, u32[]{:S(2)}) collective-permute-start(bf16[2,12,12,1024]{3,0,2,1:T(2,128)(2,1)S(1)} %copy.29), channel_id=1, source_target_pairs={{1,0},{0,1},{3,2},{2,3},{5,4},{4,5},{7,6},{6,7},{9,8},{8,9},{11,10... | collective-permute-start | bytes 1769480 | tf_op jit(solution)/shard_map/ppermute | solution.py:15
Sparse Core Ops, SparseCore 0:
  8.9 60.9 all-gather.1
where the time goes:
time: 175 us; the launch traced here: 174 us
  waiting for transfers between devices  73.1 us (42%)
  local copies, waits for them, and re-layouts  40.6 us (23%)
  matrix products  26.7 us (15%)
  between operations  19.9 us (11%)
  starting transfers between devices  9.77 us (6%)
  other arithmetic  4.29 us (2%)
    ppermute x4, waiting for transfers between devices, from_behind(): return lax.ppermute(block, axis, route)  46.3 us
    all_gather x1, waiting for transfers between devices, local(): all_weights = lax.all_gather(weights, 'batch', axis=0, tiled=True)  26.1 us
    ppermute x4, starting transfers between devices, from_behind(): return lax.ppermute(block, axis, route)  9.77 us
    sub x1, matrix products, attend(): expsc = jnp.exp(scores - largest)  8.82 us
    transpose x1, local copies, waits for them, and re-layouts, windows(): field = field.transpose(0, 2, 4, 1, 3, 5, 6)  7.79 us
    reshape x1, local copies, waits for them, and re-layouts, windows(): return field.reshape(-1, WLEV * WLAT * WLON, features)  7.66 us
    dot_general x1, matrix products, attend(): jnp.dot(normed.reshape(-1, width), all_weights[:, :3 * width], preferred_...  6.98 us
    dot_general x1, matrix products, attend(): jnp.einsum('whqk,wkhe->wqhe', attn_probs, values_all, preferred_element_t...  6.52 us
  transfers between devices with their start and end apart: 5, of which 5 were waited for; matrix products, arithmetic and copies ran while one was open for 3% of the time, Pallas kernels for 0%

commit v1 on v0

--- a/solution.py
+++ b/solution.py
@@ -1,3 +1,4 @@
+import functools
 import jax
 import jax.numpy as jnp
 from jax import lax
@@ -7,6 +8,39 @@
 WLEV = 2
 WLAT = 6
 WLON = 12
+
+
+def pack_vectors(incoming_x, dim_i):
+    side_arr = list(incoming_x.shape[1:])
+    side_arr[dim_i] *= incoming_x.shape[0]
+    carry_out = jnp.moveaxis(incoming_x, 0, dim_i).reshape(side_arr)
+    return carry_out
+
+
+def draw_core_up(array_in, axis_name, k_dim):
+    num = lax.axis_size(axis_name)
+    pool = [(dev_j, (dev_j + 1) % num) for dev_j in range(num)]
+    part_next, e_now = ([], [])
+    shelf = [(i0, h) for h, i0 in pool]
+    s = 0
+    while s < num - 1:
+        if s % 2 == 0:
+            everything = lax.ppermute(part_next[-1] if part_next else array_in, axis_name, pool)
+            part_next.append(everything)
+        else:
+            ready = lax.ppermute(e_now[-1] if e_now else array_in, axis_name, shelf)
+            e_now.append(ready)
+        s += 1
+    upper = jnp.stack([*part_next[::-1], array_in, *e_now])
+    base_arr = len(part_next)
+    passed = lax.axis_index(axis_name)
+    tmp = passed - base_arr
+    upper = upper[(jnp.arange(num) - tmp) % num]
+    current_value = pack_vectors(upper, k_dim)
+    return current_value
+
+
+map_shards_up = functools.partial(draw_core_up, axis_name="batch", k_dim=0)
 
 
 def from_behind(block, axis, distance):
@@ -90,7 +124,7 @@
 
 def local(tokens, weights, regions, offsets):
     width = weights.shape[1] // 4
-    all_weights = lax.all_gather(weights, "batch", axis=0, tiled=True)
+    all_weights = map_shards_up(weights)
     block_in = tokens[0]
     rolled = roll_forward(block_in, offsets)
     attended = attend(layer_norm(rolled), all_weights, regions)

time: 175 us -> 196 us (1.12)
  local copies, waits for them, and re-layouts: 40.6 us -> 57.4 us
  between operations: 19.9 us -> 6.13 us
  other arithmetic: 4.29 us -> 16.7 us
  starting transfers between devices: 9.77 us -> 14.4 us
    ppermute x0 -> x3, waiting for transfers between devices: none -> 36.6 us  [the longest x2 36.6 us: draw_core_up(): lax.ppermute(part_next[-1] if part_next else array_in, axis_name, pool)]
    all_gather x1 -> x0, waiting for transfers between devices: 26.1 us -> none  [local(): all_weights = lax.all_gather(weights, 'batch', axis=0, tiled=True)]
    gather x0 -> x3, local copies, waits for them, and re-layouts: none -> 13.8 us  [draw_core_up(): upper = upper[(jnp.arange(num) - tmp) % num]]
    ppermute x4, waiting for transfers between devices: 46.3 us -> 37.5 us  [from_behind(): return lax.ppermute(block, axis, route)]
    unnamed x0 -> x1, other arithmetic: none -> 7.86 us
    ppermute x0 -> x3, starting transfers between devices: none -> 3.73 us  [the longest x2 2.26 us: draw_core_up(): lax.ppermute(part_next[-1] if part_next else array_in, axis_name, pool)]
    another operation x0 -> x1, other arithmetic: none -> 3.33 us  [draw_core_up(): upper = jnp.stack([*part_next[::-1], array_in, *e_now])]
  transfers between devices with their start and end apart: 5 -> 7, of which waited for: 5 -> 5; matrix products, arithmetic and copies ran while one was open for 3% -> 5% of each run, Pallas kernels for 0% -> 0%
where the time goes in v1:
time: 196 us; the launch traced here: 195 us
  waiting for transfers between devices  74.1 us (38%)
  local copies, waits for them, and re-layouts  57.4 us (29%)
  matrix products  26.7 us (14%)
  other arithmetic  16.7 us (9%)
  starting transfers between devices  14.4 us (7%)
  between operations  6.13 us (3%)
    ppermute x4, waiting for transfers between devices, from_behind(): return lax.ppermute(block, axis, route)  37.5 us
    ppermute x2, waiting for transfers between devices, draw_core_up(): lax.ppermute(part_next[-1] if part_next else array_in, axis_name, pool)  36.6 us
    gather x3, local copies, waits for them, and re-layouts, draw_core_up(): upper = upper[(jnp.arange(num) - tmp) % num]  13.8 us
    ppermute x4, starting transfers between devices, from_behind(): return lax.ppermute(block, axis, route)  10.7 us
    sub x1, matrix products, attend(): expsc = jnp.exp(scores - largest)  8.83 us
    unnamed x1, other arithmetic  7.86 us
    transpose x1, local copies, waits for them, and re-layouts, windows(): field = field.transpose(0, 2, 4, 1, 3, 5, 6)  7.79 us
    reshape x1, local copies, waits for them, and re-layouts, windows(): return field.reshape(-1, WLEV * WLAT * WLON, features)  7.66 us
  transfers between devices with their start and end apart: 7, of which 5 were waited for; matrix products, arithmetic and copies ran while one was open for 5% of the time, Pallas kernels for 0%

profile of v1, /device:TPU:0, one launch (start us, length us, event | category | flops | bytes accessed | tf_op | source)
XLA Modules:
  0.0 195.5 jit_solution(5786486419297205219)
XLA Ops:
  1.6 4.7 %collective-permute-start = (bf16[2,6,24,1024]{3,2,1,0:T(8,128)(2,1)S(1)}, bf16[2,6,24,1024]{3,2,1,0:T(8,128)(2,1)}, u32[]{:S(2)}, u32[]{:S(2)}) collective-permute-start(bf16[2,6,24,1024]{3,2,1,0:T(8,128)(2,1)S(1)} %slice.50), channel_id=1, source_target_pairs={{2,0},{4,2},{6,4},{0,6},{3,1},{5,3},{7,5},{1,7},{10,8},{12,10},{14... | collective-permute-start | bytes 1769480 | tf_op jit(solution)/shard_map/ppermute | solution.py:49
  6.2 1.5 collective-permute-start.4
  7.7 34.0 %collective-permute-done.2 = bf16[256,4096]{1,0:T(8,128)(2,1)S(1)} collective-permute-done((bf16[256,4096]{1,0:T(8,128)(2,1)}, bf16[256,4096]{1,0:T(8,128)(2,1)S(1)}, u32[]{:S(2)}, u32[]{:S(2)}) %collective-permute-start.2) | collective-permute-done | bytes 2097184 | tf_op jit(solution)/shard_map/ppermute | solution.py:28
  41.6 1.8 collective-permute-start.3
  46.5 1.6 fusion.18
  48.1 1.4 copy.17
  49.5 1.5 collective-permute-start.1
  54.0 10.6 %collective-permute-done.1 = bf16[2,12,12,1024]{3,0,2,1:T(2,128)(2,1)} collective-permute-done((bf16[2,12,12,1024]{3,0,2,1:T(2,128)(2,1)}, bf16[2,12,12,1024]{3,0,2,1:T(2,128)(2,1)}, u32[]{:S(2)}, u32[]{:S(2)}) %collective-permute-start.1) | collective-permute-done | bytes 589856 | tf_op jit(solution)/shard_map/ppermute | solution.py:49
  67.3 1.4 fusion.14
  68.7 2.7 %collective-permute-done.3 = bf16[256,4096]{1,0:T(8,128)(2,1)} collective-permute-done((bf16[256,4096]{1,0:T(8,128)(2,1)S(1)}, bf16[256,4096]{1,0:T(8,128)(2,1)}, u32[]{:S(2)}, u32[]{:S(2)}) %collective-permute-start.3) | collective-permute-done | bytes 2097184 | tf_op jit(solution)/shard_map/ppermute | solution.py:28
  71.4 3.3 %pad_maximum_fusion = bf16[4,256,4096]{2,1,0:T(8,128)(2,1)S(1)} fusion(bf16[1,256,4096]{2,1,0:T(8,128)(2,1)} %bitcast.7, bf16[1,256,4096]{2,1,0:T(8,128)(2,1)S(1)} %bitcast.60, bf16[1,256,4096]{2,1,0:T(8,128)(2,1)S(1)} %bitcast.61, bf16[1,256,4096]{2,1,0:T(8,128)(2,1)} %bitcast.4), kind=kLoop, calls=%fused_computation.6 | loop fusion | flops 12582912 | bytes 16777216 | tf_op jit(solution)/shard_map/stack | solution.py:34
  74.7 3.8 %fusion.31 = (bf16[4,256,2048]{2,1,0:T(8,128)(2,1)}, bf16[4,256,2048]{2,1,0:T(8,128)(2,1)}) fusion(bf16[4,256,4096]{2,1,0:T(8,128)(2,1)S(1)} %pad_maximum_fusion), kind=kLoop, calls=%fused_computation.55 | loop fusion | bytes 16777216 | tf_op jit(solution)/shard_map/gather | solution.py:38
  78.5 4.9 %gather_fusion = bf16[4,256,2048]{2,1,0:T(8,128)(2,1)} fusion(bf16[4,256,2048]{2,1,0:T(8,128)(2,1)} %get-tuple-element.7, s32[1024]{0:T(1024)S(1)} %pad_clamp_fusion), kind=kCustom, calls=%fused_computation | custom fusion | bytes 8388624 | tf_op jit(solution)/shard_map/gather | solution.py:38
  83.5 5.0 %gather_fusion.1 = bf16[4,256,2048]{2,1,0:T(8,128)(2,1)} fusion(bf16[4,256,2048]{2,1,0:T(8,128)(2,1)} %get-tuple-element.8, s32[1024]{0:T(1024)S(1)} %pad_clamp_fusion), kind=kCustom, calls=%fused_computation.1 | custom fusion | bytes 8388624 | tf_op jit(solution)/shard_map/gather | solution.py:38
  88.5 7.9 %pad_maximum_fusion.1 = bf16[4,256,4096]{2,1,0:T(8,128)(2,1)} fusion(bf16[4,256,2048]{2,1,0:T(8,128)(2,1)} %gather_fusion.1, bf16[4,256,2048]{2,1,0:T(8,128)(2,1)} %gather_fusion), kind=kLoop, calls=%fused_computation.7 | loop fusion | flops 16777216 | bytes 16777216
  96.3 7.0 %fusion.8 = bf16[576,3072]{1,0:T(8,128)(2,1)S(1)} fusion(bf16[576,1024]{1,0:T(8,128)(2,1)} %bitcast.62, bf16[1024,4096]{1,0:T(8,128)(2,1)} %bitcast.51), kind=kOutput, calls=%fused_computation.15 | convolution fusion | flops 3625648128 | bytes 11010048 | tf_op jit(solution)/shard_map/dot_general | solution.py:80
  103.3 3.4 %reshape_reshape.6 = bf16[1,2,2,6,2,12,3072]{6,5,4,3,2,1,0:T(8,128)(2,1)} reshape(bf16[576,3072]{1,0:T(8,128)(2,1)S(1)} %fusion.8) | data formatting | bytes 7077888 | tf_op jit(solution)/shard_map/reshape;reshape | solution.py:62
  106.7 7.8 %copy.19 = bf16[1,2,2,2,6,12,3072]{6,2,1,5,4,3,0:T(2,128)(2,1)} copy(bf16[1,2,2,2,6,12,3072]{6,5,2,4,1,3,0:T(8,128)(2,1)} %bitcast.50) | data formatting | bytes 7077888 | tf_op jit(solution)/shard_map/transpose | solution.py:65
  114.5 7.7 %reshape.98 = bf16[4,144,3072]{2,0,1:T(4,128)(2,1)S(1)} reshape(bf16[1,2,2,2,6,12,3072]{6,2,1,5,4,3,0:T(2,128)(2,1)} %copy.19) | data formatting | bytes 7077888 | tf_op jit(solution)/shard_map/reshape | solution.py:66
  122.1 2.7 %fusion.32 = (bf16[4,144,1024]{2,0,1:T(4,128)(2,1)}, bf16[4,144,1024]{2,0,1:T(4,128)(2,1)}, bf16[4,144,1024]{2,0,1:T(4,128)(2,1)}) fusion(bf16[4,144,3072]{2,0,1:T(4,128)(2,1)S(1)} %reshape.98), kind=kLoop, calls=%fused_computation.56 | loop fusion | bytes 7077888 | tf_op jit(solution)/shard_map/slice | solution.py:87
  124.8 4.1 %copy.22 = bf16[4,144,1024]{1,2,0:T(8,128)(2,1)} copy(bf16[4,144,1024]{2,0,1:T(4,128)(2,1)} %get-tuple-element.10) | data formatting | bytes 2359296 | tf_op jit(solution)/shard_map/slice | solution.py:86
  128.9 2.5 %copy.23 = bf16[4,144,1024]{1,2,0:T(8,128)(2,1)} copy(bf16[4,144,1024]{2,0,1:T(4,128)(2,1)S(1)} %copy-done.1) | data formatting | bytes 2359296 | tf_op jit(solution)/shard_map/slice | solution.py:87
  131.4 2.5 %copy.20 = bf16[4,144,1024]{1,2,0:T(8,128)(2,1)} copy(bf16[4,144,1024]{2,0,1:T(4,128)(2,1)S(1)} %copy-done) | data formatting | bytes 2359296 | tf_op jit(solution)/shard_map/slice | solution.py:88
  133.9 8.8 %fusion.34 = (f32[4,16,144]{2,1,0:T(8,128)S(1)}, f32[4,16,144,144]{2,3,1,0:T(8,128)}) fusion(pred[4,144,144]{1,2,0:T(8,128)(4,1)S(1)} %copy-done.5, bf16[4,144,16,64]{1,3,2,0:T(8,128)(2,1)S(1)} %bitcast.57, bf16[4,144,16,64]{1,3,2,0:T(8,128)(2,1)} %bitcast.58), kind=kOutput, calls=%fused_computation.58 | convolution fusion | flops 175177872 | bytes 7787520 | tf_op jit(solution)/shard_map/sub | solution.py:96
  142.7 6.5 %convert_bitcast_fusion = bf16[4,144,16,64]{1,3,2,0:T(8,128)(2,1)} fusion(bf16[4,144,16,64]{1,3,2,0:T(8,128)(2,1)} %bitcast.59, f32[4,16,144,144]{2,3,1,0:T(8,128)} %get-tuple-element.15, f32[4,16,144]{2,1,0:T(8,128)S(1)} %get-tuple-element.14), kind=kOutput, calls=%fused_computation.25 | convolution fusion | flops 173113344 | bytes 7704576 | tf_op jit(solution)/shard_map/whqk,wkhe->wqhe/dot_general | solution.py:98
  149.3 3.8 %copy.25 = bf16[4,144,16,64]{3,2,0,1:T(8,128)(2,1)S(1)} copy(bf16[4,144,16,64]{1,3,2,0:T(8,128)(2,1)} %convert_bitcast_fusion) | data formatting | bytes 2359296 | tf_op jit(solution)/shard_map/convert_element_type | solution.py:101
  153.0 1.4 reshape_reshape.7
  156.1 2.4 %collective-permute-start.5 = (bf16[2,6,24,1024]{3,2,1,0:T(8,128)(2,1)S(1)}, bf16[2,6,24,1024]{3,2,1,0:T(8,128)(2,1)S(1)}, u32[]{:S(2)}, u32[]{:S(2)}) collective-permute-start(bf16[2,6,24,1024]{3,2,1,0:T(8,128)(2,1)S(1)} %slice.56), channel_id=1, source_target_pairs={{6,0},{0,2},{2,4},{4,6},{7,1},{1,3},{3,5},{5,7},{14,8},{8,10},{10,... | collective-permute-start | bytes 1769480 | tf_op jit(solution)/shard_map/ppermute | solution.py:49
  159.6 14.4 %collective-permute-done.5 = bf16[2,6,24,1024]{3,2,1,0:T(8,128)(2,1)S(1)} collective-permute-done((bf16[2,6,24,1024]{3,2,1,0:T(8,128)(2,1)S(1)}, bf16[2,6,24,1024]{3,2,1,0:T(8,128)(2,1)S(1)}, u32[]{:S(2)}, u32[]{:S(2)}) %collective-permute-start.5) | collective-permute-done | bytes 589856 | tf_op jit(solution)/shard_map/ppermute | solution.py:49
  175.1 2.1 %collective-permute-start.6 = (bf16[2,12,12,1024]{3,0,2,1:T(2,128)(2,1)S(1)}, bf16[2,12,12,1024]{3,0,2,1:T(2,128)(2,1)S(1)}, u32[]{:S(2)}, u32[]{:S(2)}) collective-permute-start(bf16[2,12,12,1024]{3,0,2,1:T(2,128)(2,1)S(1)} %copy.29), channel_id=1, source_target_pairs={{1,0},{0,1},{3,2},{2,3},{5,4},{4,5},{7,6},{6,7},{9,8},{8,9},{11,10... | collective-permute-start | bytes 1769480 | tf_op jit(solution)/shard_map/ppermute | solution.py:49
  178.4 12.5 %collective-permute-done.6 = bf16[2,12,12,1024]{3,0,2,1:T(2,128)(2,1)S(1)} collective-permute-done((bf16[2,12,12,1024]{3,0,2,1:T(2,128)(2,1)S(1)}, bf16[2,12,12,1024]{3,0,2,1:T(2,128)(2,1)S(1)}, u32[]{:S(2)}, u32[]{:S(2)}) %collective-permute-start.6) | collective-permute-done | bytes 589856 | tf_op jit(solution)/shard_map/ppermute | solution.py:49
  191.1 4.3 %fusion.16 = bf16[1,2,12,24,1024]{4,3,2,1,0:T(8,128)(2,1)} fusion(bf16[1024,4096]{1,0:T(8,128)(2,1)} %bitcast.52, s32[]{:T(128)S(6)} %select_n.46, bf16[2,12,12,1024]{3,2,1,0:T(8,128)(2,1)S(1)} %copy.30, bf16[2,12,24,1024]{3,2,1,0:T(8,128)(2,1)S(1)} %fusion.17, bf16[1,2,12,24,1024]{4,3,2,1,0:T(8,128)(2,1)S(1)} %copy-done.2), kind=kOutput, calls=%fused_computation.34 | convolution fusion | flops 1212088320 | bytes 6225924 | tf_op jit(solution)/shard_map/dot_general | solution.py:132
  (38 shorter events, 9.6 us)
Async XLA Ops:
  0.0 41.6 %collective-permute-start.2 = (bf16[256,4096]{1,0:T(8,128)(2,1)}, bf16[256,4096]{1,0:T(8,128)(2,1)S(1)}, u32[]{:S(2)}, u32[]{:S(2)}) collective-permute-start(bf16[256,4096]{1,0:T(8,128)(2,1)} %param.5), channel_id=1, source_target_pairs={{0,8},{8,16},{16,24},{24,0},{1,9},{9,17},{17,25},{25,1},{2,10},{10... | collective-permute-start | bytes 6291464 | tf_op jit(solution)/shard_map/ppermute | solution.py:28
  1.6 44.9 %collective-permute-start = (bf16[2,6,24,1024]{3,2,1,0:T(8,128)(2,1)S(1)}, bf16[2,6,24,1024]{3,2,1,0:T(8,128)(2,1)}, u32[]{:S(2)}, u32[]{:S(2)}) collective-permute-start(bf16[2,6,24,1024]{3,2,1,0:T(8,128)(2,1)S(1)} %slice.50), channel_id=1, source_target_pairs={{2,0},{4,2},{6,4},{0,6},{3,1},{5,3},{7,5},{1,7},{10,8},{12,10},{14... | collective-permute-start | bytes 1769480 | tf_op jit(solution)/shard_map/ppermute | solution.py:49
  6.2 62.5 %collective-permute-start.4 = (bf16[256,4096]{1,0:T(8,128)(2,1)}, bf16[256,4096]{1,0:T(8,128)(2,1)}, u32[]{:S(2)}, u32[]{:S(2)}) collective-permute-start(bf16[256,4096]{1,0:T(8,128)(2,1)} %param.5), channel_id=1, source_target_pairs={{8,0},{16,8},{24,16},{0,24},{9,1},{17,9},{25,17},{1,25},{10,2},{18... | collective-permute-start | bytes 6291464 | tf_op jit(solution)/shard_map/ppermute | solution.py:31
  41.6 29.7 %collective-permute-start.3 = (bf16[256,4096]{1,0:T(8,128)(2,1)S(1)}, bf16[256,4096]{1,0:T(8,128)(2,1)}, u32[]{:S(2)}, u32[]{:S(2)}) collective-permute-start(bf16[256,4096]{1,0:T(8,128)(2,1)S(1)} %collective-permute-done.2), channel_id=1, source_target_pairs={{0,8},{8,16},{16,24},{24,0},{1,9},{9,17},{17,25},{25,1},{2,10},{10... | collective-permute-start | bytes 6291464 | tf_op jit(solution)/shard_map/ppermute | solution.py:28
  46.4 5.9 %copy-start.6 = (s32[2,12,24]{2,0,1:T(2,128)S(1)}, s32[2,12,24]{2,0,1:T(2,128)}, u32[]{:S(2)}) copy-start(s32[2,12,24]{2,0,1:T(2,128)} %param.6) | copy-start | bytes 6916
  49.5 15.1 %collective-permute-start.1 = (bf16[2,12,12,1024]{3,0,2,1:T(2,128)(2,1)}, bf16[2,12,12,1024]{3,0,2,1:T(2,128)(2,1)}, u32[]{:S(2)}, u32[]{:S(2)}) collective-permute-start(bf16[2,12,12,1024]{3,0,2,1:T(2,128)(2,1)} %copy.17), channel_id=1, source_target_pairs={{1,0},{0,1},{3,2},{2,3},{5,4},{4,5},{7,6},{6,7},{9,8},{8,9},{11,10... | collective-permute-start | bytes 1769480 | tf_op jit(solution)/shard_map/ppermute | solution.py:49
  66.8 4.5 %copy-start.4 = (bf16[256,4096]{1,0:T(8,128)(2,1)S(1)}, bf16[256,4096]{1,0:T(8,128)(2,1)}, u32[]{:S(2)}) copy-start(bf16[256,4096]{1,0:T(8,128)(2,1)} %param.5) | copy-start | bytes 6291460
  124.8 4.1 %copy-start.1 = (bf16[4,144,1024]{2,0,1:T(4,128)(2,1)S(1)}, bf16[4,144,1024]{2,0,1:T(4,128)(2,1)}, u32[]{:S(2)}) copy-start(bf16[4,144,1024]{2,0,1:T(4,128)(2,1)} %get-tuple-element.9) | copy-start | bytes 3538948
  128.9 2.5 %copy-start = (bf16[4,144,1024]{2,0,1:T(4,128)(2,1)S(1)}, bf16[4,144,1024]{2,0,1:T(4,128)(2,1)}, u32[]{:S(2)}) copy-start(bf16[4,144,1024]{2,0,1:T(4,128)(2,1)} %get-tuple-element.11) | copy-start | bytes 3538948
  131.4 2.5 %copy-start.3 = (bf16[4,144,1024]{1,2,0:T(8,128)(2,1)S(1)}, bf16[4,144,1024]{1,2,0:T(8,128)(2,1)}, u32[]{:S(2)}) copy-start(bf16[4,144,1024]{1,2,0:T(8,128)(2,1)} %copy.22) | copy-start | bytes 3538948
  131.4 2.5 %copy-start.5 = (pred[4,144,144]{1,2,0:T(8,128)(4,1)S(1)}, pred[4,144,144]{1,2,0:T(8,128)(4,1)}, u32[]{:S(2)}) copy-start(pred[4,144,144]{1,2,0:T(8,128)(4,1)} %broadcast_compare_fusion) | copy-start | bytes 248836
  156.1 17.9 %collective-permute-start.5 = (bf16[2,6,24,1024]{3,2,1,0:T(8,128)(2,1)S(1)}, bf16[2,6,24,1024]{3,2,1,0:T(8,128)(2,1)S(1)}, u32[]{:S(2)}, u32[]{:S(2)}) collective-permute-start(bf16[2,6,24,1024]{3,2,1,0:T(8,128)(2,1)S(1)} %slice.56), channel_id=1, source_target_pairs={{6,0},{0,2},{2,4},{4,6},{7,1},{1,3},{3,5},{5,7},{14,8},{8,10},{10,... | collective-permute-start | bytes 1769480 | tf_op jit(solution)/shard_map/ppermute | solution.py:49
  174.3 16.9 %copy-start.2 = (bf16[1,2,12,24,1024]{4,3,2,1,0:T(8,128)(2,1)S(1)}, bf16[1,2,12,24,1024]{4,3,2,1,0:T(8,128)(2,1)}, u32[]{:S(2)}) copy-start(bf16[1,2,12,24,1024]{4,3,2,1,0:T(8,128)(2,1)} %param.4) | copy-start | bytes 3538948
  175.1 15.8 %collective-permute-start.6 = (bf16[2,12,12,1024]{3,0,2,1:T(2,128)(2,1)S(1)}, bf16[2,12,12,1024]{3,0,2,1:T(2,128)(2,1)S(1)}, u32[]{:S(2)}, u32[]{:S(2)}) collective-permute-start(bf16[2,12,12,1024]{3,0,2,1:T(2,128)(2,1)S(1)} %copy.29), channel_id=1, source_target_pairs={{1,0},{0,1},{3,2},{2,3},{5,4},{4,5},{7,6},{6,7},{9,8},{8,9},{11,10... | collective-permute-start | bytes 1769480 | tf_op jit(solution)/shard_map/ppermute | solution.py:49
